TPU v7x, 32 devices: a whole 2x2x4 slice. The times are simulated.
32 devices in a mesh: dp: 1, mp: 32 (over z, y, x, core).
Axes of the slice: x: 2, y: 2, z: 4, core: 2. Of those that a mesh axis runs over, the one named last changes fastest.
Arguments:
- activations: bfloat16 [2048, 8192], P('dp', 'mp'), may hold values from -6 to 6
- w_up: bfloat16 [5, 256, 32768], P(None, None, 'mp'), may hold values from -0.15625 to 0.15625
- w_down: bfloat16 [5, 32768, 256], P(None, 'mp'), may hold values from -0.078125 to 0.078125
- u_up: bfloat16 [8192, 128], P('mp'), may hold values from -0.0625 to 0.0625
- v_up: bfloat16 [128, 32768], P(None, 'mp'), may hold values from -0.5 to 0.5
- u_down: bfloat16 [32768, 128], P('mp'), may hold values from -0.03125 to 0.03125
- v_down: bfloat16 [128, 8192], P(None, 'mp'), may hold values from -0.5 to 0.5
- mask_up: int32 [4, 32], P(None, 'mp'), may hold values 0 or 1
- mask_down: int32 [4, 32], P(None, 'mp'), may hold values 0 or 1
- grad_y: bfloat16 [2048, 8192], P('dp', 'mp'), may hold values from -6 to 6
Outputs:
- output: bfloat16 [2048, 8192], P('dp', 'mp')
- grad_x: bfloat16 [2048, 8192], P('dp', 'mp')
- grad_w_up: float32 [5, 256, 32768], P(None, None, 'mp')
- grad_w_down: float32 [5, 32768, 256], P(None, 'mp')
- grad_u_up: float32 [8192, 128], P('mp')
- grad_v_up: float32 [128, 32768], P(None, 'mp')
- grad_u_down: float32 [32768, 128], P('mp')
- grad_v_down: float32 [128, 8192], P(None, 'mp')
All inputs are finite; a program needn't handle non-finite values. No bound on the sum of `mask_up` or of `mask_down` on one device may be relied on, other than what follows from the above.
Results may differ from a plain program's by a relative error of at most 0.008.
Values may be sent and summed in bfloat16 or wider, within the bound.
A program may use at most 192 MiB of HBM per device.

v0:
```python
import functools

import jax
import jax.numpy as jnp
from jax import lax
from jax.experimental import pallas as pl
from jax.experimental.pallas import tpu as pltpu
from jax.sharding import PartitionSpec as P

CHUNKS = 4
PIECES = 4
ROWS = 256
COLUMNS = 256
ROOT = 0.7978845608028654
CUBIC = 0.044715
VMEM_LIMIT = 67043328
MESH = pl.DeviceIdType.MESH
EARLY_ISSUE = ((2, 2, 2), (0, 2, 2), (2, 0, 1), (0, 1, 0), (1, 1, 0), (1, 1, 0), (1, 1, 1), (1, 0, 2), (0, 2, 2), (2, 2, 2))
CHUNK_ISSUE = 2
LATE_ISSUE = ((0, 0, 0), (1, 1, 0), (1, 0, 1), (0, 1, 1), (1, 1, 0), (1, 1, 0), (0, 1, 1), (1, 0, 1), (2, 2, 0), (1, 1, 2))


def dot(left, right):
    return jnp.dot(left, right, preferred_element_type=jnp.float32)


def dot_nt(left, right):
    return lax.dot_general(left, right, (((1,), (1,)), ((), ())), preferred_element_type=jnp.float32)


def dot_tn(left, right):
    return lax.dot_general(left, right, (((0,), (0,)), ((), ())), preferred_element_type=jnp.float32)


class Sum:
    def __init__(self, me, order, acc, sent, got, held, send_sems, recv_sems):
        self.me, self.order = me, order
        self.acc, self.sent, self.got, self.held = acc, sent, got, held
        self.send_sems, self.recv_sems = send_sems, recv_sems
        self.base, self.length, self.offset = jnp.int32(0), acc.shape[0], 0
        self.rounds = len(order)
        self.copy = None

    def bit(self, level):
        return lax.rem(lax.div(self.me, jnp.int32(1 << level)), jnp.int32(2))

    def rows(self, base, length):
        return pl.ds(pl.multiple_of(base, length), length)

    def remote(self, src, dst, step, level):
        self.copy = pltpu.make_async_remote_copy(
            src_ref=src, dst_ref=dst, send_sem=self.send_sems.at[step], recv_sem=self.recv_sems.at[step],
            device_id={"mp": partner(self.me, level)}, device_id_type=MESH,
        )
        self.copy.start()

    def start(self, step):
        if step < self.rounds:
            level = self.order[step]
            half = self.length // 2
            bit = self.bit(level)
            here = pl.ds(self.offset, half)
            self.sent[here, :] = self.acc[self.rows(self.base + (1 - bit) * half, half), :].astype(jnp.bfloat16)
            self.remote(self.sent.at[here], self.got.at[here], step, level)
        else:
            level = self.order[2 * self.rounds - 1 - step]
            if step == self.rounds:
                mine = self.rows(self.base, self.length)
                self.held[mine, :] = self.acc[mine, :].astype(jnp.bfloat16)
            mine = self.held.at[self.rows(self.base, self.length)]
            self.remote(mine, mine, step, level)

    def finish(self, step):
        self.copy.wait()
        if step < self.rounds:
            half = self.length // 2
            self.base = self.base + self.bit(self.order[step]) * half
            kept = self.rows(self.base, half)
            self.acc[kept, :] = self.acc[kept, :] + self.got[pl.ds(self.offset, half), :].astype(jnp.float32)
            self.offset += half
            self.length = half
        else:
            level = self.order[2 * self.rounds - 1 - step]
            self.base = self.base - self.bit(level) * self.length
            self.length *= 2


def partner(me, level):
    step = 1 << level
    bit = lax.rem(lax.div(me, jnp.int32(step)), jnp.int32(2))
    return me + (1 - 2 * bit) * step


def kernel(rounds, mu_ref, md_ref, x_hbm, gy_hbm, wu_hbm, wd_hbm, uu_hbm, vu_hbm, ud_hbm, vd_hbm,
           out_hbm, gx_hbm, gwu_hbm, gwd_hbm, guu_hbm, gvu_hbm, gud_hbm, gvd_hbm,
           xs, wu, wd, uu, vu, ud, vd, hid, gp, put, came, diag, acc, zs, zl, sent_e, got_e, sent_l, got_l,
           stage_up, stage_down, out_v, gx_v, guu, gvu, gud, gvd, mask_mine, mask_theirs,
           load_sems, mask_send, mask_recv, in_send, in_recv, put_send, put_recv, es, er, ls, lr, store_sems):
    slabs, tokens = xs.shape[:2]
    levels = slabs - 1
    width, hidden = wu.shape[1:]
    rank = vu.shape[0]
    chunk = tokens // CHUNKS
    piece = chunk // PIECES
    pieces = CHUNKS * PIECES
    step = min(COLUMNS, hidden)
    me = lax.axis_index("mp")

    loads = []
    for i, (src, dst) in enumerate((
        (x_hbm, xs.at[0, :, pl.ds(0, width)]), (gy_hbm, xs.at[0, :, pl.ds(width, width)]),
        (uu_hbm, uu), (vd_hbm, vd), (wu_hbm, wu), (wd_hbm, wd), (vu_hbm, vu), (ud_hbm, ud),
    )):
        loads.append(pltpu.make_async_copy(src, dst, load_sems.at[i]))
        loads[-1].start()

    barrier = pltpu.get_barrier_semaphore()
    for level in range(rounds):
        pl.semaphore_signal(barrier, inc=1, device_id={"mp": partner(me, level)}, device_id_type=MESH)
    for k in range(levels):
        mask_mine[8 * k:8 * k + 8, :] = jnp.full((8, 128), md_ref[k].astype(jnp.float32))
    pl.semaphore_wait(barrier, rounds)

    def mask_copy(k):
        here = pl.ds(8 * k, 8)
        return pltpu.make_async_remote_copy(
            src_ref=mask_mine.at[here], dst_ref=mask_theirs.at[here], send_sem=mask_send.at[k], recv_sem=mask_recv.at[k],
            device_id={"mp": partner(me, k)}, device_id_type=MESH)

    def input_copy(k, start, length):
        rows = pl.ds(start, length)
        return pltpu.make_async_remote_copy(
            src_ref=xs.at[0, rows], dst_ref=xs.at[k + 1, rows], send_sem=in_send.at[k], recv_sem=in_recv.at[k, lax.div(start, chunk)],
            device_id={"mp": partner(me, k)}, device_id_type=MESH)

    def partial_copy(k, start, length):
        rows = pl.ds(start, length)
        return pltpu.make_async_remote_copy(
            src_ref=put.at[k, rows], dst_ref=came.at[k, rows], send_sem=put_send.at[k], recv_sem=put_recv.at[k, lax.div(start, chunk)],
            device_id={"mp": partner(me, k)}, device_id_type=MESH)

    in_done = [0] * levels
    put_done = [0] * levels

    def issue(copy, done, k, count):
        for i in range(done[k], min(pieces, done[k] + count)):
            copy(k, i * piece, piece).start()
        done[k] = min(pieces, done[k] + count)

    loads[0].wait()
    loads[1].wait()
    for k in range(levels):
        mask_copy(k).start()
    issue(input_copy, in_done, 0, PIECES)
    for k in range(1, levels):
        issue(input_copy, in_done, k, EARLY_ISSUE[0][k - 1])
    loads[2].wait()
    loads[3].wait()

    @pl.loop(0, CHUNKS)
    def _(c):
        rows = pl.ds(pl.multiple_of(c * chunk, chunk), chunk)
        acc[rows, :rank] = dot(xs[0, rows, :width], uu[...])
        acc[rows, rank:] = dot_nt(xs[0, rows, width:], vd[...])

    early = Sum(me, tuple(range(rounds)), acc, sent_e, got_e, zs, es, er)
    for s in range(2 * rounds):
        early.start(s)
        if s == 0:
            issue(input_copy, in_done, 0, pieces)
        elif s < len(EARLY_ISSUE):
            for k in range(1, levels):
                issue(input_copy, in_done, k, EARLY_ISSUE[s][k - 1])
        if s == 0:
            loads[4].wait()
            for k in range(levels):
                wu[k + 1] = (wu[k + 1].astype(jnp.float32) * mu_ref[k].astype(jnp.float32)).astype(jnp.bfloat16)
        if s == 1:
            loads[5].wait()
            for k in range(levels):
                mask_copy(k).wait()
                row = jnp.concatenate([mask_theirs[8 * k:8 * k + 1, :]] * (width // 128), axis=1)
                wd[k + 1] = (wd[k + 1].astype(jnp.float32) * row).astype(jnp.bfloat16)
        if s == 2:
            loads[6].wait()
            loads[7].wait()
        early.finish(s)
    for k in range(1, levels):
        issue(input_copy, in_done, k, pieces)

    @pl.loop(0, CHUNKS)
    def _(c):
        for k in range(levels):
            input_copy(k, c * chunk, chunk).wait_recv()

        @pl.loop(0, chunk // ROWS)
        def _(r):
            rows = pl.ds(pl.multiple_of(c * chunk + r * ROWS, ROWS), ROWS)
            for start in range(0, hidden, step):
                cols = slice(start, start + step)
                v = dot(zs[rows, :rank], vu[:, cols])
                gh = dot_nt(zs[rows, rank:], ud[cols, :])
                for k in range(slabs):
                    v += dot(xs[k, rows, :width], wu[k, :, cols])
                    gh += dot_nt(xs[k, rows, width:], wd[k, cols, :])
                square = v * v
                half_tanh = 0.5 * jnp.tanh(v * (ROOT + (ROOT * CUBIC) * square))
                gate = 0.5 + half_tanh
                hid[rows, cols] = (v * gate).astype(jnp.bfloat16)
                slope = gate + v * (0.5 - 2.0 * half_tanh * half_tanh) * (ROOT + (3.0 * ROOT * CUBIC) * square)
                gp[rows, cols] = (gh * slope).astype(jnp.bfloat16)
            h = hid[rows, :]
            g = gp[rows, :]
            for k in range(levels):
                put[k, rows, :width] = dot(h, wd[k + 1]).astype(jnp.bfloat16)
                put[k, rows, width:] = dot_nt(g, wu[k + 1]).astype(jnp.bfloat16)
            acc[rows, :rank] = dot(h, ud[...])
            acc[rows, rank:] = dot_nt(g, vu[...])
            diag[rows, :width] = dot(h, wd[0])
            diag[rows, width:] = dot_nt(g, wu[0])

        partial_copy(0, c * chunk, chunk).start()
        for k in range(1, levels):
            for i in range(CHUNK_ISSUE):
                partial_copy(k, (c * CHUNK_ISSUE + i) * piece, piece).start()

    for k in range(levels):
        put_done[k] = pieces if k == 0 else CHUNKS * CHUNK_ISSUE

    stores = []

    def store(src, dst):
        stores.append(pltpu.make_async_copy(src, dst, store_sems.at[len(stores)]))
        stores[-1].start()
        return stores[-1]

    held = [None, None]
    pending = []

    def slab_grads(k):
        slot = k % 2
        if held[slot]:
            for copy in held[slot]:
                copy.wait()
                pending.remove(copy)
        for start in range(0, width, ROWS):
            stop = min(width, start + ROWS)
            up = dot_tn(xs[k, :, start:stop], gp[...])
            if k:
                up = up * mu_ref[k - 1].astype(jnp.float32)
            stage_up[slot, start:stop, :] = up

        @pl.loop(0, hidden // step)
        def _(b):
            cols = pl.ds(pl.multiple_of(b * step, step), step)
            down = dot_tn(hid[:, cols], xs[k, :, width:])
            if k:
                down = down * jnp.concatenate([mask_theirs[8 * k - 8:8 * k - 7, :]] * (width // 128), axis=1)
            stage_down[slot, cols, :] = down

        held[slot] = (store(stage_up.at[slot], gwu_hbm.at[k]), store(stage_down.at[slot], gwd_hbm.at[k]))
        pending.extend(held[slot])

    late = Sum(me, (0,) + tuple(range(levels - 1, 0, -1)) + tuple(range(levels, rounds)), acc, sent_l, got_l, zl, ls, lr)
    for s in range(2 * rounds):
        late.start(s)
        if s < len(LATE_ISSUE):
            for k in range(1, levels):
                issue(partial_copy, put_done, k, LATE_ISSUE[s][k - 1])
        if 1 <= s <= slabs:
            slab_grads(s - 1)
        if s == slabs + 1:
            gvu[...] = dot_tn(zs[:, :rank], gp[...])
            pending.append(store(gvu, gvu_hbm))
            gud[...] = dot_tn(hid[...], zs[:, rank:])
            pending.append(store(gud, gud_hbm))
        late.finish(s)
    for k in range(1, levels):
        issue(partial_copy, put_done, k, pieces)

    guu[...] = dot_tn(xs[0, :, :width], zl[:, rank:])
    pending.append(store(guu, guu_hbm))
    gvd[...] = dot_tn(zl[:, :rank], xs[0, :, width:])
    pending.append(store(gvd, gvd_hbm))

    for c in range(CHUNKS):
        rows = pl.ds(c * chunk, chunk)
        out = diag[rows, :width] + dot(zl[rows, :rank], vd[...])
        gx = diag[rows, width:] + dot_nt(zl[rows, rank:], uu[...])
        for k in range(levels):
            partial_copy(k, c * chunk, chunk).wait_recv()
            out = out + came[k, rows, :width].astype(jnp.float32)
            gx = gx + came[k, rows, width:].astype(jnp.float32)
        out_v[rows, :] = out.astype(jnp.bfloat16)
        gx_v[rows, :] = gx.astype(jnp.bfloat16)
        pending.append(store(out_v.at[rows], out_hbm.at[rows]))
        pending.append(store(gx_v.at[rows], gx_hbm.at[rows]))
    for copy in pending:
        copy.wait()
    for k in range(levels):
        input_copy(k, 0, tokens).wait_send()
        partial_copy(k, 0, tokens).wait_send()


def summed_over_dp(array):
    if lax.axis_size("dp") == 1:
        return array
    return lax.psum(array.astype(jnp.bfloat16), "dp").astype(jnp.float32)


def per_device(activations, w_up, w_down, u_up, v_up, u_down, v_down, mask_up, mask_down, grad_y):
    bf, f32 = jnp.bfloat16, jnp.float32
    slabs, width, hidden = w_up.shape
    tokens = activations.shape[0]
    rank = v_up.shape[0]
    levels = slabs - 1
    rounds = lax.axis_size("mp").bit_length() - 1
    vmem = pltpu.VMEM
    dma = lambda *shape: pltpu.SemaphoreType.DMA(shape)
    shape = jax.ShapeDtypeStruct
    outs = [
        shape((tokens, width), bf), shape((tokens, width), bf), shape((slabs, width, hidden), f32), shape((slabs, hidden, width), f32),
        shape((width, rank), f32), shape((rank, hidden), f32), shape((hidden, rank), f32), shape((rank, width), f32),
    ]
    scratch = [
        vmem((slabs, tokens, 2 * width), bf), vmem(w_up.shape, bf), vmem(w_down.shape, bf),
        vmem(u_up.shape, bf), vmem(v_up.shape, bf), vmem(u_down.shape, bf), vmem(v_down.shape, bf),
        vmem((tokens, hidden), bf), vmem((tokens, hidden), bf),
        vmem((levels, tokens, 2 * width), bf), vmem((levels, tokens, 2 * width), bf), vmem((tokens, 2 * width), f32),
        vmem((tokens, 2 * rank), f32), vmem((tokens, 2 * rank), bf), vmem((tokens, 2 * rank), bf),
        vmem((tokens, 2 * rank), bf), vmem((tokens, 2 * rank), bf), vmem((tokens, 2 * rank), bf), vmem((tokens, 2 * rank), bf),
        vmem((2, width, hidden), f32), vmem((2, hidden, width), f32), vmem((tokens, width), bf), vmem((tokens, width), bf),
        vmem((width, rank), f32), vmem((rank, hidden), f32), vmem((hidden, rank), f32), vmem((rank, width), f32),
        vmem((8 * levels, 128), f32), vmem((8 * levels, 128), f32),
        dma(8), dma(levels), dma(levels), dma(levels), dma(levels, CHUNKS), dma(levels), dma(levels, CHUNKS),
        dma(2 * rounds), dma(2 * rounds), dma(2 * rounds), dma(2 * rounds), dma(2 * slabs + 4 + 2 * CHUNKS),
    ]
    smem = pl.BlockSpec(memory_space=pltpu.SMEM)
    hbm = pl.BlockSpec(memory_space=pl.ANY)
    got = pl.pallas_call(
        functools.partial(kernel, rounds),
        in_specs=[smem, smem] + [hbm] * 8,
        out_specs=[hbm] * len(outs),
        out_shape=outs,
        scratch_shapes=scratch,
        compiler_params=pltpu.CompilerParams(vmem_limit_bytes=VMEM_LIMIT, collective_id=0, has_side_effects=True),
        name="sublayer",
    )(mask_up[:, 0], mask_down[:, 0], activations, grad_y, w_up, w_down, u_up, v_up, u_down, v_down)
    return tuple(got[:2]) + tuple(summed_over_dp(g) for g in got[2:])


def solution(mesh):
    acts, rows, columns = P("dp", "mp"), P("mp", None), P(None, "mp")
    up, down = P(None, None, "mp"), P(None, "mp", None)
    return jax.shard_map(
        per_device,
        mesh=mesh,
        in_specs=(acts, up, down, rows, columns, rows, columns, columns, columns, acts),
        out_specs=(acts, acts, up, down, rows, columns, rows, columns),
        check_vma=False,
    )
```

profile of v0, /device:TPU:0, one launch (start us, length us, event | category | flops | bytes accessed | tf_op | source)
XLA Modules:
  0.0 154.6 jit_solution(14987548480669808668)
XLA Ops:
  0.6 138.1 %sublayer.1 = (bf16[2048,256]{1,0:T(8,128)(2,1)}, bf16[2048,256]{1,0:T(8,128)(2,1)}, f32[5,256,1024]{2,1,0:T(8,128)}, f32[5,1024,256]{2,1,0:T(8,128)}, f32[256,1...) custom-call(s32[4]{0:T(128)} %bitcast.4, s32[4]{0:T(128)} %bitcast.5, ...), custom_call_target="tpu_custom_call" | custom-call | tf_op jit(solution)/shard_map/sublayer/pallas_call | solution.py:340
  138.8 2.3 %copy.26 = bf16[2048,256]{1,0:T(8,128)(2,1)} copy(bf16[2048,256]{1,0:T(8,128)(2,1)} %get-tuple-element.16) | data formatting | bytes 2097152
  141.0 0.0 slice-start
  141.0 2.4 %copy.27 = bf16[2048,256]{1,0:T(8,128)(2,1)} copy(bf16[2048,256]{1,0:T(8,128)(2,1)} %get-tuple-element.17) | data formatting | bytes 2097152
  143.5 0.0 slice-start.1
  143.5 5.8 %copy.28 = f32[5,256,1024]{2,1,0:T(8,128)} copy(f32[5,256,1024]{2,1,0:T(8,128)} %get-tuple-element.18) | data formatting | bytes 10485760
  149.2 0.0 slice-done
  149.2 0.0 slice-done.1
  149.3 0.0 copy-start.3
  149.3 0.0 copy-start.1
  149.3 0.0 copy-start
  149.3 0.0 copy-start.2
  149.3 2.4 %copy.29 = f32[5,1024,256]{2,1,0:T(8,128)} copy(f32[5,1024,256]{2,1,0:T(8,128)S(1)} %bitcast.3) | data formatting | bytes 10485760
  151.6 0.0 copy-done.3
  151.7 0.7 copy.30
  152.3 0.0 copy-done.1
  152.3 0.8 copy.31
  153.1 0.0 copy-done
  153.1 0.8 copy.32
  153.9 0.0 copy-done.2
  153.9 0.7 copy.33
  (1 shorter events, 0.0 us)
Async XLA Ops:
  141.0 8.2 %slice-start = ((s8[5242880]{0:T(1024)(128)(4,1)}), s8[4194304]{0:T(1024)(128)(4,1)S(1)}, s32[]{:S(2)}) async-start(s8[5242880]{0:T(1024)(128)(4,1)} %bitcast.2), calls=%async_computation | async-start | bytes 8388608
  143.5 5.8 %slice-start.1 = ((s8[5242880]{0:T(1024)(128)(4,1)}), s8[1048576]{0:T(1024)(128)(4,1)S(1)}, s32[]{:S(2)}) async-start(s8[5242880]{0:T(1024)(128)(4,1)} %bitcast.2), calls=%async_computation.1 | async-start | bytes 2097152
  149.3 2.4 %copy-start.3 = (f32[256,128]{1,0:T(8,128)S(1)}, f32[256,128]{1,0:T(8,128)}, u32[]{:S(2)}) copy-start(f32[256,128]{1,0:T(8,128)} %get-tuple-element.20) | copy-start | bytes 393220
  149.3 3.1 %copy-start.1 = (f32[128,1024]{1,0:T(8,128)S(1)}, f32[128,1024]{1,0:T(8,128)}, u32[]{:S(2)}) copy-start(f32[128,1024]{1,0:T(8,128)} %get-tuple-element.21) | copy-start | bytes 1572868
  149.3 3.8 %copy-start = (f32[1024,128]{1,0:T(8,128)S(1)}, f32[1024,128]{1,0:T(8,128)}, u32[]{:S(2)}) copy-start(f32[1024,128]{1,0:T(8,128)} %get-tuple-element.22) | copy-start | bytes 1572868
  149.3 4.6 %copy-start.2 = (f32[128,256]{1,0:T(8,128)S(1)}, f32[128,256]{1,0:T(8,128)}, u32[]{:S(2)}) copy-start(f32[128,256]{1,0:T(8,128)} %get-tuple-element.23) | copy-start | bytes 393220
where the time goes:
time: 155 us
  Pallas kernels  138 us (89%)
  local copies, waits for them, and re-layouts  15.7 us (10%)
    pallas_call x1, Pallas kernels, per_device(): pl.pallas_call(functools.partial(kernel, rounds), in_specs=[smem, smem] +...  138 us
    unnamed x20, local copies, waits for them, and re-layouts  15.7 us

commit v1 on v0

--- a/solution.py
+++ b/solution.py
@@ -9,15 +9,20 @@
 
 CHUNKS = 4
 PIECES = 4
+PARTS = 2
+AHEAD = 2
+AHEAD_AT = (7, 9)
 ROWS = 256
 COLUMNS = 256
 ROOT = 0.7978845608028654
 CUBIC = 0.044715
 VMEM_LIMIT = 67043328
 MESH = pl.DeviceIdType.MESH
-EARLY_ISSUE = ((2, 2, 2), (0, 2, 2), (2, 0, 1), (0, 1, 0), (1, 1, 0), (1, 1, 0), (1, 1, 1), (1, 0, 2), (0, 2, 2), (2, 2, 2))
-CHUNK_ISSUE = 2
-LATE_ISSUE = ((0, 0, 0), (1, 1, 0), (1, 0, 1), (0, 1, 1), (1, 1, 0), (1, 1, 0), (0, 1, 1), (1, 0, 1), (2, 2, 0), (1, 1, 2))
+EARLY_ORDERS = ((0, 1, 2, 3), (0, 2, 3, 1))
+LATE_ORDERS = ((0, 2, 3, 1), (0, 1, 2, 3))
+EARLY_ISSUE = ((1, 1, 2), (1, 0, 0), (0, 2, 0), (1, 1, 0), (1, 1, 1), (1, 0, 1), (0, 1, 1), (1, 1, 2), (2, 2, 2))
+CHUNK_ISSUE = ((2, 2, 2), (2, 2, 2), (0, 1, 2), (0, 0, 0))
+LATE_ISSUE = ((1, 0, 1), (0, 1, 1), (1, 1, 1), (1, 1, 1), (2, 1, 1), (0, 1, 1), (1, 1, 0), (1, 1, 1), (2, 2, 2))
 
 
 def dot(left, right):
@@ -33,12 +38,15 @@
 
 
 class Sum:
-    def __init__(self, me, order, acc, sent, got, held, send_sems, recv_sems):
-        self.me, self.order = me, order
+    def __init__(self, me, part, order, acc, sent, got, held, send_sems, recv_sems, apart):
+        self.me, self.part, self.order = me, part, order
         self.acc, self.sent, self.got, self.held = acc, sent, got, held
         self.send_sems, self.recv_sems = send_sems, recv_sems
-        self.base, self.length, self.offset = jnp.int32(0), acc.shape[0], 0
+        self.length = acc.shape[0] // PARTS
+        self.base, self.offset = jnp.int32(part * self.length), part * self.length
         self.rounds = len(order)
+        self.steps = 2 * self.rounds - 1
+        self.landing = acc.shape[0] + part * (self.length >> self.rounds - 1) if apart else None
         self.copy = None
 
     def bit(self, level):
@@ -49,40 +57,52 @@
 
     def remote(self, src, dst, step, level):
         self.copy = pltpu.make_async_remote_copy(
-            src_ref=src, dst_ref=dst, send_sem=self.send_sems.at[step], recv_sem=self.recv_sems.at[step],
+            src_ref=src, dst_ref=dst, send_sem=self.send_sems.at[self.part, step], recv_sem=self.recv_sems.at[self.part, step],
             device_id={"mp": partner(self.me, level)}, device_id_type=MESH,
         )
         self.copy.start()
 
+    def landed(self, step, size):
+        last = step == self.rounds - 1 and self.landing is not None
+        return pl.ds(self.landing if last else self.offset, size)
+
     def start(self, step):
         if step < self.rounds:
             level = self.order[step]
-            half = self.length // 2
-            bit = self.bit(level)
-            here = pl.ds(self.offset, half)
-            self.sent[here, :] = self.acc[self.rows(self.base + (1 - bit) * half, half), :].astype(jnp.bfloat16)
-            self.remote(self.sent.at[here], self.got.at[here], step, level)
+            last = step == self.rounds - 1
+            size = self.length if last else self.length // 2
+            base = self.base if last else self.base + (1 - self.bit(level)) * size
+            here = pl.ds(self.offset, size)
+            self.sent[here, :] = self.acc[self.rows(base, size), :].astype(jnp.bfloat16)
+            self.remote(self.sent.at[here], self.got.at[self.landed(step, size)], step, level)
         else:
-            level = self.order[2 * self.rounds - 1 - step]
-            if step == self.rounds:
-                mine = self.rows(self.base, self.length)
-                self.held[mine, :] = self.acc[mine, :].astype(jnp.bfloat16)
             mine = self.held.at[self.rows(self.base, self.length)]
-            self.remote(mine, mine, step, level)
+            self.remote(mine, mine, step, self.order[self.steps - 1 - step])
 
     def finish(self, step):
         self.copy.wait()
         if step < self.rounds:
-            half = self.length // 2
-            self.base = self.base + self.bit(self.order[step]) * half
-            kept = self.rows(self.base, half)
-            self.acc[kept, :] = self.acc[kept, :] + self.got[pl.ds(self.offset, half), :].astype(jnp.float32)
-            self.offset += half
-            self.length = half
+            last = step == self.rounds - 1
+            size = self.length if last else self.length // 2
+            if not last:
+                self.base = self.base + self.bit(self.order[step]) * size
+            kept = self.rows(self.base, size)
+            total = self.acc[kept, :] + self.got[self.landed(step, size), :].astype(jnp.float32)
+            if last:
+                self.held[kept, :] = total.astype(jnp.bfloat16)
+            else:
+                self.acc[kept, :] = total
+            self.offset += size
+            self.length = size
         else:
-            level = self.order[2 * self.rounds - 1 - step]
-            self.base = self.base - self.bit(level) * self.length
+            self.base = self.base - self.bit(self.order[self.steps - 1 - step]) * self.length
             self.length *= 2
+
+    def advance(self, step):
+        if step > 0:
+            self.finish(step - 1)
+        if step < self.steps:
+            self.start(step)
 
 
 def partner(me, level):
@@ -93,8 +113,8 @@
 
 def kernel(rounds, mu_ref, md_ref, x_hbm, gy_hbm, wu_hbm, wd_hbm, uu_hbm, vu_hbm, ud_hbm, vd_hbm,
            out_hbm, gx_hbm, gwu_hbm, gwd_hbm, guu_hbm, gvu_hbm, gud_hbm, gvd_hbm,
-           xs, wu, wd, uu, vu, ud, vd, hid, gp, put, came, diag, acc, zs, zl, sent_e, got_e, sent_l, got_l,
-           stage_up, stage_down, out_v, gx_v, guu, gvu, gud, gvd, mask_mine, mask_theirs,
+           xs, wu, wd, uu, vu, ud, vd, hid, gp, put, came, diag, acc, zs, zl, sent, got,
+           pre, gh_sum, guu, gvd, mask_mine, mask_theirs,
            load_sems, mask_send, mask_recv, in_send, in_recv, put_send, put_recv, es, er, ls, lr, store_sems):
     slabs, tokens = xs.shape[:2]
     levels = slabs - 1
@@ -163,9 +183,33 @@
         acc[rows, :rank] = dot(xs[0, rows, :width], uu[...])
         acc[rows, rank:] = dot_nt(xs[0, rows, width:], vd[...])
 
-    early = Sum(me, tuple(range(rounds)), acc, sent_e, got_e, zs, es, er)
+    def sums(rows, start):
+        cols = slice(start, start + step)
+        v = dot(xs[0, rows, :width], wu[0, :, cols])
+        gh = dot_nt(xs[0, rows, width:], wd[0, cols, :])
+        for k in range(1, slabs):
+            v += dot(xs[k, rows, :width], wu[k, :, cols])
+            gh += dot_nt(xs[k, rows, width:], wd[k, cols, :])
+        return v, gh
+
+    def sums_ahead(c):
+        for k in range(levels):
+            input_copy(k, c * chunk, chunk).wait_recv()
+
+        @pl.loop(0, chunk // ROWS)
+        def _(r):
+            rows = pl.ds(pl.multiple_of(c * chunk + r * ROWS, ROWS), ROWS)
+            for start in range(0, hidden, step):
+                pre[rows, start:start + step], gh_sum[rows, start:start + step] = sums(rows, start)
+
+    tail = tuple(range(levels, rounds))
+    early = [
+        Sum(me, 0, EARLY_ORDERS[0] + tail, acc, sent, got, zs, es, er, False),
+        Sum(me, 1, EARLY_ORDERS[1] + tail, acc, sent, got, zs, es, er, False),
+    ]
     for s in range(2 * rounds):
-        early.start(s)
+        for part in early:
+            part.advance(s)
         if s == 0:
             issue(input_copy, in_done, 0, pieces)
         elif s < len(EARLY_ISSUE):
@@ -184,25 +228,20 @@
         if s == 2:
             loads[6].wait()
             loads[7].wait()
-        early.finish(s)
+        if s in AHEAD_AT:
+            sums_ahead(AHEAD_AT.index(s))
     for k in range(1, levels):
         issue(input_copy, in_done, k, pieces)
 
-    @pl.loop(0, CHUNKS)
-    def _(c):
-        for k in range(levels):
-            input_copy(k, c * chunk, chunk).wait_recv()
-
+    def products(c, chunks, ahead):
         @pl.loop(0, chunk // ROWS)
         def _(r):
             rows = pl.ds(pl.multiple_of(c * chunk + r * ROWS, ROWS), ROWS)
             for start in range(0, hidden, step):
                 cols = slice(start, start + step)
-                v = dot(zs[rows, :rank], vu[:, cols])
-                gh = dot_nt(zs[rows, rank:], ud[cols, :])
-                for k in range(slabs):
-                    v += dot(xs[k, rows, :width], wu[k, :, cols])
-                    gh += dot_nt(xs[k, rows, width:], wd[k, cols, :])
+                v, gh = (pre[rows, cols], gh_sum[rows, cols]) if ahead else sums(rows, start)
+                v += dot(zs[rows, :rank], vu[:, cols])
+                gh += dot_nt(zs[rows, rank:], ud[cols, :])
                 square = v * v
                 half_tanh = 0.5 * jnp.tanh(v * (ROOT + (ROOT * CUBIC) * square))
                 gate = 0.5 + half_tanh
@@ -221,11 +260,26 @@
 
         partial_copy(0, c * chunk, chunk).start()
         for k in range(1, levels):
-            for i in range(CHUNK_ISSUE):
-                partial_copy(k, (c * CHUNK_ISSUE + i) * piece, piece).start()
+            for at in chunks:
+                first = sum(row[k - 1] for row in CHUNK_ISSUE[:at])
+
+                @pl.when(c == at)
+                def _():
+                    for i in range(first, first + CHUNK_ISSUE[at][k - 1]):
+                        partial_copy(k, i * piece, piece).start()
+
+    @pl.loop(0, AHEAD)
+    def _(c):
+        products(c, range(AHEAD), True)
+
+    @pl.loop(AHEAD, CHUNKS)
+    def _(c):
+        for k in range(levels):
+            input_copy(k, c * chunk, chunk).wait_recv()
+        products(c, range(AHEAD, CHUNKS), False)
 
     for k in range(levels):
-        put_done[k] = pieces if k == 0 else CHUNKS * CHUNK_ISSUE
+        put_done[k] = pieces if k == 0 else sum(row[k - 1] for row in CHUNK_ISSUE)
 
     stores = []
 
@@ -248,7 +302,7 @@
             up = dot_tn(xs[k, :, start:stop], gp[...])
             if k:
                 up = up * mu_ref[k - 1].astype(jnp.float32)
-            stage_up[slot, start:stop, :] = up
+            pre[slot * width + start:slot * width + stop, :] = up
 
         @pl.loop(0, hidden // step)
         def _(b):
@@ -256,25 +310,30 @@
             down = dot_tn(hid[:, cols], xs[k, :, width:])
             if k:
                 down = down * jnp.concatenate([mask_theirs[8 * k - 8:8 * k - 7, :]] * (width // 128), axis=1)
-            stage_down[slot, cols, :] = down
-
-        held[slot] = (store(stage_up.at[slot], gwu_hbm.at[k]), store(stage_down.at[slot], gwd_hbm.at[k]))
+            gh_sum[cols, slot * width:(slot + 1) * width] = down
+
+        held[slot] = (store(pre.at[pl.ds(slot * width, width)], gwu_hbm.at[k]), store(gh_sum.at[pl.ds(0, hidden), pl.ds(slot * width, width)], gwd_hbm.at[k]))
         pending.extend(held[slot])
 
-    late = Sum(me, (0,) + tuple(range(levels - 1, 0, -1)) + tuple(range(levels, rounds)), acc, sent_l, got_l, zl, ls, lr)
+    late = [
+        Sum(me, 0, LATE_ORDERS[0] + tail, acc, sent, got, zl, ls, lr, True),
+        Sum(me, 1, LATE_ORDERS[1] + tail, acc, sent, got, zl, ls, lr, True),
+    ]
     for s in range(2 * rounds):
-        late.start(s)
+        for part in late:
+            part.advance(s)
         if s < len(LATE_ISSUE):
             for k in range(1, levels):
                 issue(partial_copy, put_done, k, LATE_ISSUE[s][k - 1])
         if 1 <= s <= slabs:
             slab_grads(s - 1)
         if s == slabs + 1:
+            gvu = pre.at[pl.ds(2 * width, rank)]
             gvu[...] = dot_tn(zs[:, :rank], gp[...])
             pending.append(store(gvu, gvu_hbm))
+            gud = gh_sum.at[pl.ds(0, hidden), pl.ds(2 * width, rank)]
             gud[...] = dot_tn(hid[...], zs[:, rank:])
             pending.append(store(gud, gud_hbm))
-        late.finish(s)
     for k in range(1, levels):
         issue(partial_copy, put_done, k, pieces)
 
@@ -291,15 +350,54 @@
             partial_copy(k, c * chunk, chunk).wait_recv()
             out = out + came[k, rows, :width].astype(jnp.float32)
             gx = gx + came[k, rows, width:].astype(jnp.float32)
-        out_v[rows, :] = out.astype(jnp.bfloat16)
-        gx_v[rows, :] = gx.astype(jnp.bfloat16)
-        pending.append(store(out_v.at[rows], out_hbm.at[rows]))
-        pending.append(store(gx_v.at[rows], gx_hbm.at[rows]))
+        hid[rows, :width] = out.astype(jnp.bfloat16)
+        hid[rows, width:2 * width] = gx.astype(jnp.bfloat16)
+        pending.append(store(hid.at[rows, pl.ds(0, width)], out_hbm.at[rows]))
+        pending.append(store(hid.at[rows, pl.ds(width, width)], gx_hbm.at[rows]))
     for copy in pending:
         copy.wait()
     for k in range(levels):
         input_copy(k, 0, tokens).wait_send()
         partial_copy(k, 0, tokens).wait_send()
+
+
+def settle_kernel(count, *refs):
+    sources, targets, buffers = refs[:count], refs[count:2 * count], refs[2 * count:3 * count]
+    get_sems, set_sems = refs[3 * count:]
+    moves = []
+    for source, target, buffer in zip(sources, targets, buffers):
+        views = [()] if len(source.shape) == 2 else [(i,) for i in range(source.shape[0])]
+        for view in views:
+            at = lambda ref, view=view: ref.at[view] if view else ref
+            i = len(moves)
+            moves.append((
+                pltpu.make_async_copy(at(source), at(buffer), get_sems.at[i]),
+                pltpu.make_async_copy(at(buffer), at(target), set_sems.at[i]),
+            ))
+    for get, _ in moves:
+        get.start()
+    for get, put in moves:
+        get.wait()
+        put.start()
+    for _, put in moves:
+        put.wait()
+
+
+def settled(arrays):
+    count = len(arrays)
+    moves = sum(a.shape[0] if a.ndim == 3 else 1 for a in arrays)
+    size = sum(a.size * a.dtype.itemsize for a in arrays)
+    hbm = pl.BlockSpec(memory_space=pl.ANY)
+    return pl.pallas_call(
+        functools.partial(settle_kernel, count),
+        in_specs=[hbm] * count,
+        out_specs=[hbm] * count,
+        out_shape=[jax.ShapeDtypeStruct(a.shape, a.dtype) for a in arrays],
+        scratch_shapes=[pltpu.VMEM(a.shape, a.dtype) for a in arrays] + [pltpu.SemaphoreType.DMA((moves,))] * 2,
+        compiler_params=pltpu.CompilerParams(vmem_limit_bytes=VMEM_LIMIT),
+        cost_estimate=pl.CostEstimate(flops=0, bytes_accessed=2 * size, transcendentals=0),
+        name="settle",
+    )(*arrays)
 
 
 def summed_over_dp(array):
@@ -328,12 +426,12 @@
         vmem((tokens, hidden), bf), vmem((tokens, hidden), bf),
         vmem((levels, tokens, 2 * width), bf), vmem((levels, tokens, 2 * width), bf), vmem((tokens, 2 * width), f32),
         vmem((tokens, 2 * rank), f32), vmem((tokens, 2 * rank), bf), vmem((tokens, 2 * rank), bf),
-        vmem((tokens, 2 * rank), bf), vmem((tokens, 2 * rank), bf), vmem((tokens, 2 * rank), bf), vmem((tokens, 2 * rank), bf),
-        vmem((2, width, hidden), f32), vmem((2, hidden, width), f32), vmem((tokens, width), bf), vmem((tokens, width), bf),
-        vmem((width, rank), f32), vmem((rank, hidden), f32), vmem((hidden, rank), f32), vmem((rank, width), f32),
+        vmem((tokens, 2 * rank), bf), vmem((tokens + (tokens >> rounds - 1), 2 * rank), bf),
+        vmem((AHEAD * tokens // CHUNKS, hidden), f32), vmem((AHEAD * tokens // CHUNKS, hidden), f32),
+        vmem((width, rank), f32), vmem((rank, width), f32),
         vmem((8 * levels, 128), f32), vmem((8 * levels, 128), f32),
         dma(8), dma(levels), dma(levels), dma(levels), dma(levels, CHUNKS), dma(levels), dma(levels, CHUNKS),
-        dma(2 * rounds), dma(2 * rounds), dma(2 * rounds), dma(2 * rounds), dma(2 * slabs + 4 + 2 * CHUNKS),
+        dma(PARTS, 2 * rounds - 1), dma(PARTS, 2 * rounds - 1), dma(PARTS, 2 * rounds - 1), dma(PARTS, 2 * rounds - 1), dma(2 * slabs + 4 + 2 * CHUNKS),
     ]
     smem = pl.BlockSpec(memory_space=pltpu.SMEM)
     hbm = pl.BlockSpec(memory_space=pl.ANY)
@@ -346,6 +444,7 @@
         compiler_params=pltpu.CompilerParams(vmem_limit_bytes=VMEM_LIMIT, collective_id=0, has_side_effects=True),
         name="sublayer",
     )(mask_up[:, 0], mask_down[:, 0], activations, grad_y, w_up, w_down, u_up, v_up, u_down, v_down)
+    got = settled(got)
     return tuple(got[:2]) + tuple(summed_over_dp(g) for g in got[2:])
 
 

time: 155 us -> 138 us (0.89)
  local copies, waits for them, and re-layouts: 15.7 us -> 0 us
    unnamed x20 -> x0, local copies, waits for them, and re-layouts: 15.7 us -> none
    pallas_call x1, Pallas kernels: 138 us -> 128 us  [per_device(): pl.pallas_call(functools.partial(kernel, rounds), in_specs=[smem, smem] +...]
    pallas_call x0 -> x1, Pallas kernels: none -> 9.9 us  [settled(): pl.pallas_call(functools.partial(settle_kernel, count), in_specs=[hbm] *...]
where the time goes in v1:
time: 138 us
  Pallas kernels  137 us (99%)
    pallas_call x1, Pallas kernels, per_device(): pl.pallas_call(functools.partial(kernel, rounds), in_specs=[smem, smem] +...  128 us
    pallas_call x1, Pallas kernels, settled(): pl.pallas_call(functools.partial(settle_kernel, count), in_specs=[hbm] *...  9.9 us

profile of v1, /device:TPU:0, one launch (start us, length us, event | category | flops | bytes accessed | tf_op | source)
XLA Modules:
  0.0 138.3 jit_solution(6736536125711076183)
XLA Ops:
  0.6 127.6 %sublayer.1 = (bf16[2048,256]{1,0:T(8,128)(2,1)}, bf16[2048,256]{1,0:T(8,128)(2,1)}, f32[5,256,1024]{2,1,0:T(8,128)}, f32[5,1024,256]{2,1,0:T(8,128)}, f32[256,1...) custom-call(s32[4]{0:T(128)} %bitcast.2, s32[4]{0:T(128)} %bitcast.3, ...), custom_call_target="tpu_custom_call" | custom-call | tf_op jit(solution)/shard_map/sublayer/pallas_call | solution.py:438
  128.2 9.9 %settle.1 = (bf16[2048,256]{1,0:T(8,128)(2,1)}, bf16[2048,256]{1,0:T(8,128)(2,1)}, f32[5,256,1024]{2,1,0:T(8,128)}, f32[5,1024,256]{2,1,0:T(8,128)}, f32[256,128...) custom-call(bf16[2048,256]{1,0:T(8,128)(2,1)} %get-tuple-element.16.refs_0_, ...), custom_call_target="tpu_custom_call" | custom-call | bytes 27787264 | tf_op jit(solution)/shard_map/settle/pallas_call | solution.py:391

commit v2 on v1

--- a/solution.py
+++ b/solution.py
@@ -1,4 +1,5 @@
 import functools
+import math
 
 import jax
 import jax.numpy as jnp
@@ -11,7 +12,8 @@
 PIECES = 4
 PARTS = 2
 AHEAD = 2
-AHEAD_AT = (7, 9)
+AHEAD_AT = (6, 8)
+SLOTS = 4
 ROWS = 256
 COLUMNS = 256
 ROOT = 0.7978845608028654
@@ -22,7 +24,7 @@
 LATE_ORDERS = ((0, 2, 3, 1), (0, 1, 2, 3))
 EARLY_ISSUE = ((1, 1, 2), (1, 0, 0), (0, 2, 0), (1, 1, 0), (1, 1, 1), (1, 0, 1), (0, 1, 1), (1, 1, 2), (2, 2, 2))
 CHUNK_ISSUE = ((2, 2, 2), (2, 2, 2), (0, 1, 2), (0, 0, 0))
-LATE_ISSUE = ((1, 0, 1), (0, 1, 1), (1, 1, 1), (1, 1, 1), (2, 1, 1), (0, 1, 1), (1, 1, 0), (1, 1, 1), (2, 2, 2))
+LATE_ISSUE = ((2, 1, 1), (1, 1, 1), (1, 1, 1), (1, 2, 1), (2, 1, 2), (1, 1, 1), (1, 1, 1), (2, 2, 2), (4, 4, 4))
 
 
 def dot(left, right):
@@ -112,10 +114,9 @@
 
 
 def kernel(rounds, mu_ref, md_ref, x_hbm, gy_hbm, wu_hbm, wd_hbm, uu_hbm, vu_hbm, ud_hbm, vd_hbm,
-           out_hbm, gx_hbm, gwu_hbm, gwd_hbm, guu_hbm, gvu_hbm, gud_hbm, gvd_hbm,
-           xs, wu, wd, uu, vu, ud, vd, hid, gp, put, came, diag, acc, zs, zl, sent, got,
-           pre, gh_sum, guu, gvd, mask_mine, mask_theirs,
-           load_sems, mask_send, mask_recv, in_send, in_recv, put_send, put_recv, es, er, ls, lr, store_sems):
+           pre, gh_sum, acc, hid, guu, gvd, gvu, gud,
+           xs, wu, wd, uu, vu, ud, vd, gp, put, came, diag, zs, zl, sent, got, mask_mine, mask_theirs,
+           load_sems, mask_send, mask_recv, in_send, in_recv, put_send, put_recv, es, er, ls, lr):
     slabs, tokens = xs.shape[:2]
     levels = slabs - 1
     width, hidden = wu.shape[1:]
@@ -281,28 +282,18 @@
     for k in range(levels):
         put_done[k] = pieces if k == 0 else sum(row[k - 1] for row in CHUNK_ISSUE)
 
-    stores = []
-
-    def store(src, dst):
-        stores.append(pltpu.make_async_copy(src, dst, store_sems.at[len(stores)]))
-        stores[-1].start()
-        return stores[-1]
-
-    held = [None, None]
-    pending = []
-
     def slab_grads(k):
-        slot = k % 2
-        if held[slot]:
-            for copy in held[slot]:
-                copy.wait()
-                pending.remove(copy)
         for start in range(0, width, ROWS):
             stop = min(width, start + ROWS)
             up = dot_tn(xs[k, :, start:stop], gp[...])
             if k:
                 up = up * mu_ref[k - 1].astype(jnp.float32)
-            pre[slot * width + start:slot * width + stop, :] = up
+            if k < SLOTS:
+                pre[k * width + start:k * width + stop, :] = up
+            else:
+                for j in range(hidden // (2 * rank)):
+                    base = hidden + j * width
+                    acc[base + start:base + stop, :] = up[:, j * 2 * rank:(j + 1) * 2 * rank]
 
         @pl.loop(0, hidden // step)
         def _(b):
@@ -310,10 +301,14 @@
             down = dot_tn(hid[:, cols], xs[k, :, width:])
             if k:
                 down = down * jnp.concatenate([mask_theirs[8 * k - 8:8 * k - 7, :]] * (width // 128), axis=1)
-            gh_sum[cols, slot * width:(slot + 1) * width] = down
-
-        held[slot] = (store(pre.at[pl.ds(slot * width, width)], gwu_hbm.at[k]), store(gh_sum.at[pl.ds(0, hidden), pl.ds(slot * width, width)], gwd_hbm.at[k]))
-        pending.extend(held[slot])
+            if k < SLOTS:
+                gh_sum[cols, k * width:(k + 1) * width] = down
+            else:
+                acc[cols, :width] = down
+
+    def rank_grads():
+        gvu[...] = dot_tn(zs[:, :rank], gp[...])
+        gud[...] = dot_tn(hid[...], zs[:, rank:])
 
     late = [
         Sum(me, 0, LATE_ORDERS[0] + tail, acc, sent, got, zl, ls, lr, True),
@@ -325,22 +320,17 @@
         if s < len(LATE_ISSUE):
             for k in range(1, levels):
                 issue(partial_copy, put_done, k, LATE_ISSUE[s][k - 1])
-        if 1 <= s <= slabs:
-            slab_grads(s - 1)
-        if s == slabs + 1:
-            gvu = pre.at[pl.ds(2 * width, rank)]
-            gvu[...] = dot_tn(zs[:, :rank], gp[...])
-            pending.append(store(gvu, gvu_hbm))
-            gud = gh_sum.at[pl.ds(0, hidden), pl.ds(2 * width, rank)]
-            gud[...] = dot_tn(hid[...], zs[:, rank:])
-            pending.append(store(gud, gud_hbm))
+        if s < SLOTS:
+            slab_grads(s)
+        if s == rounds:
+            rank_grads()
+        if s == rounds + 1:
+            slab_grads(SLOTS)
     for k in range(1, levels):
         issue(partial_copy, put_done, k, pieces)
 
     guu[...] = dot_tn(xs[0, :, :width], zl[:, rank:])
-    pending.append(store(guu, guu_hbm))
     gvd[...] = dot_tn(zl[:, :rank], xs[0, :, width:])
-    pending.append(store(gvd, gvd_hbm))
 
     for c in range(CHUNKS):
         rows = pl.ds(c * chunk, chunk)
@@ -352,52 +342,49 @@
             gx = gx + came[k, rows, width:].astype(jnp.float32)
         hid[rows, :width] = out.astype(jnp.bfloat16)
         hid[rows, width:2 * width] = gx.astype(jnp.bfloat16)
-        pending.append(store(hid.at[rows, pl.ds(0, width)], out_hbm.at[rows]))
-        pending.append(store(hid.at[rows, pl.ds(width, width)], gx_hbm.at[rows]))
-    for copy in pending:
-        copy.wait()
     for k in range(levels):
         input_copy(k, 0, tokens).wait_send()
         partial_copy(k, 0, tokens).wait_send()
 
 
-def settle_kernel(count, *refs):
-    sources, targets, buffers = refs[:count], refs[count:2 * count], refs[2 * count:3 * count]
-    get_sems, set_sems = refs[3 * count:]
-    moves = []
-    for source, target, buffer in zip(sources, targets, buffers):
-        views = [()] if len(source.shape) == 2 else [(i,) for i in range(source.shape[0])]
-        for view in views:
-            at = lambda ref, view=view: ref.at[view] if view else ref
-            i = len(moves)
-            moves.append((
-                pltpu.make_async_copy(at(source), at(buffer), get_sems.at[i]),
-                pltpu.make_async_copy(at(buffer), at(target), set_sems.at[i]),
-            ))
-    for get, _ in moves:
-        get.start()
-    for get, put in moves:
-        get.wait()
-        put.start()
-    for _, put in moves:
-        put.wait()
-
-
-def settled(arrays):
-    count = len(arrays)
-    moves = sum(a.shape[0] if a.ndim == 3 else 1 for a in arrays)
-    size = sum(a.size * a.dtype.itemsize for a in arrays)
-    hbm = pl.BlockSpec(memory_space=pl.ANY)
+def settle_kernel(pre, gh_sum, acc, hid, guu, gvd, gvu, gud, out, gx, gwu, gwd, guu_out, gvu_out, gud_out, gvd_out, sems):
+    slabs, width, hidden = gwu.shape
+    block = acc.shape[1]
+    pairs = []
+    for k in range(SLOTS):
+        pairs.append((pre.at[pl.ds(k * width, width)], gwu.at[k]))
+        pairs.append((gh_sum.at[pl.ds(0, hidden), pl.ds(k * width, width)], gwd.at[k]))
+    for j in range(hidden // block):
+        pairs.append((acc.at[pl.ds(hidden + j * width, width)], gwu.at[SLOTS, :, pl.ds(j * block, block)]))
+    pairs.append((acc.at[pl.ds(0, hidden), pl.ds(0, width)], gwd.at[SLOTS]))
+    pairs.append((hid.at[:, pl.ds(0, width)], out))
+    pairs.append((hid.at[:, pl.ds(width, width)], gx))
+    pairs.append((guu, guu_out))
+    pairs.append((gvd, gvd_out))
+    pairs.append((gvu, gvu_out))
+    pairs.append((gud, gud_out))
+    puts = [pltpu.make_async_copy(src, dst, sems.at[i]) for i, (src, dst) in enumerate(pairs)]
+    for copy in puts:
+        copy.start()
+    for copy in puts:
+        copy.wait()
+
+
+def settled(got, outs):
+    width, hidden = outs[2].shape[1:]
+    copies = 2 * SLOTS + hidden // got[2].shape[1] + 7
+    size = sum(a.size * a.dtype.itemsize for a in outs)
+    hbm, vmem = pl.BlockSpec(memory_space=pl.ANY), pl.BlockSpec(memory_space=pltpu.VMEM)
     return pl.pallas_call(
-        functools.partial(settle_kernel, count),
-        in_specs=[hbm] * count,
-        out_specs=[hbm] * count,
-        out_shape=[jax.ShapeDtypeStruct(a.shape, a.dtype) for a in arrays],
-        scratch_shapes=[pltpu.VMEM(a.shape, a.dtype) for a in arrays] + [pltpu.SemaphoreType.DMA((moves,))] * 2,
-        compiler_params=pltpu.CompilerParams(vmem_limit_bytes=VMEM_LIMIT),
-        cost_estimate=pl.CostEstimate(flops=0, bytes_accessed=2 * size, transcendentals=0),
+        settle_kernel,
+        in_specs=[vmem] * len(got),
+        out_specs=[hbm] * len(outs),
+        out_shape=outs,
+        scratch_shapes=[pltpu.SemaphoreType.DMA((copies,))],
+        compiler_params=pltpu.CompilerParams(vmem_limit_bytes=1024 * 1024),
+        cost_estimate=pl.CostEstimate(flops=0, bytes_accessed=size, transcendentals=0),
         name="settle",
-    )(*arrays)
+    )(*got)
 
 
 def summed_over_dp(array):
@@ -423,28 +410,31 @@
     scratch = [
         vmem((slabs, tokens, 2 * width), bf), vmem(w_up.shape, bf), vmem(w_down.shape, bf),
         vmem(u_up.shape, bf), vmem(v_up.shape, bf), vmem(u_down.shape, bf), vmem(v_down.shape, bf),
-        vmem((tokens, hidden), bf), vmem((tokens, hidden), bf),
+        vmem((tokens, hidden), bf),
         vmem((levels, tokens, 2 * width), bf), vmem((levels, tokens, 2 * width), bf), vmem((tokens, 2 * width), f32),
-        vmem((tokens, 2 * rank), f32), vmem((tokens, 2 * rank), bf), vmem((tokens, 2 * rank), bf),
+        vmem((tokens, 2 * rank), bf), vmem((tokens, 2 * rank), bf),
         vmem((tokens, 2 * rank), bf), vmem((tokens + (tokens >> rounds - 1), 2 * rank), bf),
-        vmem((AHEAD * tokens // CHUNKS, hidden), f32), vmem((AHEAD * tokens // CHUNKS, hidden), f32),
-        vmem((width, rank), f32), vmem((rank, width), f32),
         vmem((8 * levels, 128), f32), vmem((8 * levels, 128), f32),
         dma(8), dma(levels), dma(levels), dma(levels), dma(levels, CHUNKS), dma(levels), dma(levels, CHUNKS),
-        dma(PARTS, 2 * rounds - 1), dma(PARTS, 2 * rounds - 1), dma(PARTS, 2 * rounds - 1), dma(PARTS, 2 * rounds - 1), dma(2 * slabs + 4 + 2 * CHUNKS),
+        dma(PARTS, 2 * rounds - 1), dma(PARTS, 2 * rounds - 1), dma(PARTS, 2 * rounds - 1), dma(PARTS, 2 * rounds - 1),
     ]
+    left = [
+        ((AHEAD * tokens // CHUNKS, hidden), f32), ((AHEAD * tokens // CHUNKS, hidden), f32), ((tokens, 2 * rank), f32),
+        ((tokens, hidden), bf), ((width, rank), f32), ((rank, width), f32), ((rank, hidden), f32), ((hidden, rank), f32),
+    ]
+    taken = sum(math.prod(dims) * jnp.dtype(dtype).itemsize for dims, dtype in left)
     smem = pl.BlockSpec(memory_space=pltpu.SMEM)
     hbm = pl.BlockSpec(memory_space=pl.ANY)
     got = pl.pallas_call(
         functools.partial(kernel, rounds),
         in_specs=[smem, smem] + [hbm] * 8,
-        out_specs=[hbm] * len(outs),
-        out_shape=outs,
+        out_specs=[pl.BlockSpec(memory_space=vmem)] * len(left),
+        out_shape=[vmem(*spec) for spec in left],
         scratch_shapes=scratch,
-        compiler_params=pltpu.CompilerParams(vmem_limit_bytes=VMEM_LIMIT, collective_id=0, has_side_effects=True),
+        compiler_params=pltpu.CompilerParams(vmem_limit_bytes=VMEM_LIMIT - taken, collective_id=0, has_side_effects=True),
         name="sublayer",
     )(mask_up[:, 0], mask_down[:, 0], activations, grad_y, w_up, w_down, u_up, v_up, u_down, v_down)
-    got = settled(got)
+    got = settled(got, outs)
     return tuple(got[:2]) + tuple(summed_over_dp(g) for g in got[2:])
 
 

time: 138 us -> 131 us (0.949)
  Pallas kernels: 137 us -> 130 us
    pallas_call x1, Pallas kernels: 9.9 us -> 5.1 us  [settled(): pl.pallas_call(settle_kernel, in_specs=[vmem] * len(got), out_specs=[hbm]...]
    pallas_call x1, Pallas kernels: 128 us -> 125 us  [per_device(): pl.pallas_call(functools.partial(kernel, rounds), in_specs=[smem, smem] +...]
where the time goes in v2:
time: 131 us
  Pallas kernels  130 us (99%)
    pallas_call x1, Pallas kernels, per_device(): pl.pallas_call(functools.partial(kernel, rounds), in_specs=[smem, smem] +...  125 us
    pallas_call x1, Pallas kernels, settled(): pl.pallas_call(settle_kernel, in_specs=[vmem] * len(got), out_specs=[hbm]...  5.1 us

profile of v2, /device:TPU:0, one launch (start us, length us, event | category | flops | bytes accessed | tf_op | source)
XLA Modules:
  0.0 130.8 jit_solution(13905211750067738052)
XLA Ops:
  0.6 124.9 %sublayer.1 = (f32[1024,1024]{1,0:T(8,128)S(1)}, f32[1024,1024]{1,0:T(8,128)S(1)}, f32[2048,256]{1,0:T(8,128)S(1)}, bf16[2048,1024]{1,0:T(8,128)(2,1)S(1)}, f32[...) custom-call(s32[4]{0:T(128)} %bitcast.2, s32[4]{0:T(128)} %bitcast.3, ...), custom_call_target="tpu_custom_call" | custom-call | tf_op jit(solution)/shard_map/sublayer/pallas_call | solution.py:428
  125.6 5.1 %settle.1 = (bf16[2048,256]{1,0:T(8,128)(2,1)}, bf16[2048,256]{1,0:T(8,128)(2,1)}, f32[5,256,1024]{2,1,0:T(8,128)}, f32[5,1024,256]{2,1,0:T(8,128)}, f32[256,128...) custom-call(f32[1024,1024]{1,0:T(8,128)S(1)} %get-tuple-element.16.pre, ...), custom_call_target="tpu_custom_call" | custom-call | bytes 13893632 | tf_op jit(solution)/shard_map/settle/pallas_call | solution.py:378

commit v3 on v2

--- a/solution.py
+++ b/solution.py
@@ -14,6 +14,7 @@
 AHEAD = 2
 AHEAD_AT = (6, 8)
 SLOTS = 4
+FIRST_SLAB = 1
 ROWS = 256
 COLUMNS = 256
 ROOT = 0.7978845608028654
@@ -22,7 +23,7 @@
 MESH = pl.DeviceIdType.MESH
 EARLY_ORDERS = ((0, 1, 2, 3), (0, 2, 3, 1))
 LATE_ORDERS = ((0, 2, 3, 1), (0, 1, 2, 3))
-EARLY_ISSUE = ((1, 1, 2), (1, 0, 0), (0, 2, 0), (1, 1, 0), (1, 1, 1), (1, 0, 1), (0, 1, 1), (1, 1, 2), (2, 2, 2))
+EARLY_ISSUE = ((2, 1, 2), (1, 0, 1), (0, 2, 0), (1, 1, 1), (1, 1, 1), (1, 1, 1), (1, 1, 1), (1, 1, 1), (2, 2, 2))
 CHUNK_ISSUE = ((2, 2, 2), (2, 2, 2), (0, 1, 2), (0, 0, 0))
 LATE_ISSUE = ((2, 1, 1), (1, 1, 1), (1, 1, 1), (1, 2, 1), (2, 1, 2), (1, 1, 1), (1, 1, 1), (2, 2, 2), (4, 4, 4))
 
@@ -320,9 +321,9 @@
         if s < len(LATE_ISSUE):
             for k in range(1, levels):
                 issue(partial_copy, put_done, k, LATE_ISSUE[s][k - 1])
-        if s < SLOTS:
-            slab_grads(s)
-        if s == rounds:
+        if FIRST_SLAB <= s < FIRST_SLAB + SLOTS:
+            slab_grads(s - FIRST_SLAB)
+        if s == rounds + 2:
             rank_grads()
         if s == rounds + 1:
             slab_grads(SLOTS)

time: 131 us -> 128 us (0.977)
  Pallas kernels: 130 us -> 127 us
    pallas_call x1, Pallas kernels: 125 us -> 122 us  [per_device(): pl.pallas_call(functools.partial(kernel, rounds), in_specs=[smem, smem] +...]
where the time goes in v3:
time: 128 us
  Pallas kernels  127 us (99%)
    pallas_call x1, Pallas kernels, per_device(): pl.pallas_call(functools.partial(kernel, rounds), in_specs=[smem, smem] +...  122 us
    pallas_call x1, Pallas kernels, settled(): pl.pallas_call(settle_kernel, in_specs=[vmem] * len(got), out_specs=[hbm]...  5.1 us

profile of v3, /device:TPU:0, one launch (start us, length us, event | category | flops | bytes accessed | tf_op | source)
XLA Modules:
  0.0 128.0 jit_solution(1004451185016837805)
XLA Ops:
  0.6 122.1 %sublayer.1 = (f32[1024,1024]{1,0:T(8,128)S(1)}, f32[1024,1024]{1,0:T(8,128)S(1)}, f32[2048,256]{1,0:T(8,128)S(1)}, bf16[2048,1024]{1,0:T(8,128)(2,1)S(1)}, f32[...) custom-call(s32[4]{0:T(128)} %bitcast.2, s32[4]{0:T(128)} %bitcast.3, ...), custom_call_target="tpu_custom_call" | custom-call | tf_op jit(solution)/shard_map/sublayer/pallas_call | solution.py:429
  122.8 5.1 %settle.1 = (bf16[2048,256]{1,0:T(8,128)(2,1)}, bf16[2048,256]{1,0:T(8,128)(2,1)}, f32[5,256,1024]{2,1,0:T(8,128)}, f32[5,1024,256]{2,1,0:T(8,128)}, f32[256,128...) custom-call(f32[1024,1024]{1,0:T(8,128)S(1)} %get-tuple-element.16.pre, ...), custom_call_target="tpu_custom_call" | custom-call | bytes 13893632 | tf_op jit(solution)/shard_map/settle/pallas_call | solution.py:379

commit v4 on v3

--- a/solution.py
+++ b/solution.py
@@ -23,7 +23,7 @@
 MESH = pl.DeviceIdType.MESH
 EARLY_ORDERS = ((0, 1, 2, 3), (0, 2, 3, 1))
 LATE_ORDERS = ((0, 2, 3, 1), (0, 1, 2, 3))
-EARLY_ISSUE = ((2, 1, 2), (1, 0, 1), (0, 2, 0), (1, 1, 1), (1, 1, 1), (1, 1, 1), (1, 1, 1), (1, 1, 1), (2, 2, 2))
+EARLY_ISSUE = ((2, 2, 2), (1, 1, 1), (1, 2, 1), (1, 1, 1), (1, 1, 1), (1, 1, 1), (1, 1, 1), (1, 1, 1), (2, 2, 2))
 CHUNK_ISSUE = ((2, 2, 2), (2, 2, 2), (0, 1, 2), (0, 0, 0))
 LATE_ISSUE = ((2, 1, 1), (1, 1, 1), (1, 1, 1), (1, 2, 1), (2, 1, 2), (1, 1, 1), (1, 1, 1), (2, 2, 2), (4, 4, 4))
 

time: 128 us -> 125 us (0.977)
  Pallas kernels: 127 us -> 124 us
    pallas_call x1, Pallas kernels: 122 us -> 119 us  [per_device(): pl.pallas_call(functools.partial(kernel, rounds), in_specs=[smem, smem] +...]
where the time goes in v4:
time: 125 us
  Pallas kernels  124 us (99%)
    pallas_call x1, Pallas kernels, per_device(): pl.pallas_call(functools.partial(kernel, rounds), in_specs=[smem, smem] +...  119 us
    pallas_call x1, Pallas kernels, settled(): pl.pallas_call(settle_kernel, in_specs=[vmem] * len(got), out_specs=[hbm]...  5.1 us

profile of v4, /device:TPU:0, one launch (start us, length us, event | category | flops | bytes accessed | tf_op | source)
XLA Modules:
  0.0 124.5 jit_solution(1947390845050783025)
XLA Ops:
  0.6 118.6 %sublayer.1 = (f32[1024,1024]{1,0:T(8,128)S(1)}, f32[1024,1024]{1,0:T(8,128)S(1)}, f32[2048,256]{1,0:T(8,128)S(1)}, bf16[2048,1024]{1,0:T(8,128)(2,1)S(1)}, f32[...) custom-call(s32[4]{0:T(128)} %bitcast.2, s32[4]{0:T(128)} %bitcast.3, ...), custom_call_target="tpu_custom_call" | custom-call | tf_op jit(solution)/shard_map/sublayer/pallas_call | solution.py:429
  119.3 5.1 %settle.1 = (bf16[2048,256]{1,0:T(8,128)(2,1)}, bf16[2048,256]{1,0:T(8,128)(2,1)}, f32[5,256,1024]{2,1,0:T(8,128)}, f32[5,1024,256]{2,1,0:T(8,128)}, f32[256,128...) custom-call(f32[1024,1024]{1,0:T(8,128)S(1)} %get-tuple-element.16.pre, ...), custom_call_target="tpu_custom_call" | custom-call | bytes 13893632 | tf_op jit(solution)/shard_map/settle/pallas_call | solution.py:379
